TPU v7x, 32 devices: a whole 2x2x4 slice. The times are simulated.
32 devices in a mesh: row: 4 (over z), col: 8 (over y, x, core).
Axes of the slice: x: 2, y: 2, z: 4, core: 2. Of those that a mesh axis runs over, the one named last changes fastest.
Arguments:
- weight: float32 [16384, 16384], P('row', 'col'), may hold values from -0.046875 to 0.046875
- leak: float32 [16384], P('col'), may hold values from 0.1 to 1
- rates: float32 [3, 256, 16384], P(None, 'row', 'col'), may hold values from -0.95 to 0.95
- cotangent: float32 [256, 16384], P('row', 'col'), may hold values from -2 to 2
Outputs:
- grad_input: float32 [256, 16384], P('row', 'col')
- grad_weight: float32 [16384, 16384], P('row', 'col')
- grad_noise: float32 [3, 16384], P(None, 'row')
All inputs are finite; a program needn't handle non-finite values.
Results may differ from a plain program's by a relative error of at most 0.0001.
Values sent between devices are 32-bit elements; how exact they have to be, the bound alone decides.
A program may use at most 192 MiB of HBM per device.

v0:
```python
import jax
import jax.numpy as jnp
from jax import lax
from jax.sharding import PartitionSpec as P

TSTEPS = 3


def shards(weight, leak, rates, cotangent):
    n_col = lax.axis_size("col")
    own_rows = cotangent.shape[0]
    local_units = cotangent.shape[1]
    full_rates = lax.all_gather(rates, "row", axis=1, tiled=True)
    grad_weight = jnp.zeros(weight.shape, jnp.float32)
    noise_list = []
    carried = cotangent
    for step_back in range(TSTEPS - 1, -1, -1):
        scaled = leak[None, :] * carried
        spread = scaled.reshape(own_rows, local_units // n_col, n_col)
        by_col = lax.all_to_all(spread, "col", split_axis=2, concat_axis=1, tiled=True)
        by_row = lax.all_to_all(by_col, "row", split_axis=1, concat_axis=0, tiled=True)
        gathered = lax.all_gather(by_row, "col", axis=2, tiled=True)
        unit_block = gathered.reshape(gathered.shape[0], gathered.shape[1] * gathered.shape[2])
        rates_now = full_rates[step_back]
        noise_list.insert(0, jnp.sum(unit_block, axis=0))
        grad_weight = grad_weight + lax.dot_general(
            unit_block,
            rates_now,
            (((0,), (0,)), ((), ())),
            precision=lax.Precision.HIGHEST,
            preferred_element_type=jnp.float32,
        )
        partial_sum = jnp.dot(
            unit_block, weight, precision=lax.Precision.HIGHEST, preferred_element_type=jnp.float32
        )
        adjoint = lax.psum_scatter(partial_sum, "row", scatter_dimension=0, tiled=True)
        local_rates = rates[step_back]
        carried = (1.0 - leak[None, :]) * carried + (1.0 - local_rates * local_rates) * adjoint
    return (carried, grad_weight, jnp.stack(noise_list))


def solution(mesh):
    placed = (P("row", "col"), P("col"), P(None, "row", "col"), P("row", "col"))
    return jax.shard_map(
        shards,
        mesh=mesh,
        in_specs=placed,
        out_specs=(P("row", "col"), P("row", "col"), P(None, "row")),
        check_vma=False,
    )
```

profile of v0, /device:TPU:0, one launch (start us, length us, event | category | flops | bytes accessed | tf_op | source)
XLA Modules:
  0.0 634.5 jit_solution(5892808969612367369)
XLA Ops:
  7.2 1.1 broadcast_multiply_fusion.2
  8.6 0.4 copy.20
  9.0 14.7 %all_to_all.108 = f32[64,256,8]{1,0,2:T(8,128)S(1)} all-to-all(f32[64,256,8]{1,0,2:T(8,128)S(1)} %copy.20), channel_id=1, replica_groups=mesh['row'=4,'col'=8] {'col'}, dimensions={2} | all-to-all | bytes 1048576 | tf_op jit(solution)/shard_map/all_to_all | solution.py:20
  24.1 0.5 broadcast.24
  24.6 9.3 %reduce.3 = f32[2048,64]{1,0:T(8,128)S(1)} reduce(f32[2048,1,64]{2,1,0:T(1,128)S(1)} %bitcast.75, f32[]{:T(128)} %broadcast.24), dimensions={1}, to_apply=%bitcast.64.reduce_sub_computation | reduce | bytes 1048580
  33.9 0.7 reshape.48
  34.6 18.6 %all_to_all.109 = f32[4,1,32768]{2,1,0:T(1,128)S(1)} all-to-all(f32[4,1,32768]{2,1,0:T(1,128)S(1)} %reshape.48), channel_id=1, replica_groups=mesh['row'=4,'col'=8] {'row'}, dimensions={0} | all-to-all | bytes 1048576 | tf_op jit(solution)/shard_map/all_to_all | solution.py:21
  53.2 2.1 reduce.4
  55.3 1.3 reshape.49
  57.0 1.0 copy.24
  58.3 34.2 %all-gather.5.cloned.1.call-done = f32[256,512,8]{1,0,2:T(8,128)} async-done(((f32[256,512,1]{1,0,2:T(8,128)}), f32[256,512,8]{1,0,2:T(8,128)}) %all-gather.5.cloned.1.call-update) | async-done | bytes 4194320 | tf_op jit(solution)/shard_map/all_gather | solution.py:22
  92.6 5.4 copy.25
  98.0 33.9 %fusion.9 = f32[256,2048]{1,0:T(8,128)} fusion(f32[4096,2048]{1,0:T(8,128)} %param.4, f32[256,512,8]{0,2,1:T(8,128)} %copy.25), kind=kOutput, calls=%fused_computation.10 | convolution fusion | flops 25769803776 | bytes 39845888 | tf_op jit(solution)/shard_map/dot_general | solution.py:33
  132.0 43.7 %reduce-scatter.4.cloned.1.call-done = f32[64,2048]{1,0:T(8,128)} async-done(((f32[256,2048]{1,0:T(8,128)}), f32[64,2048]{1,0:T(8,128)}) %reduce-scatter.4.cloned.1.call-update) | async-done | bytes 524304 | tf_op jit(solution)/shard_map/reduce_scatter | solution.py:36
  175.7 1.3 broadcast_multiply_fusion.1
  177.7 13.7 %all_to_all.110 = f32[64,256,8]{1,0,2:T(8,128)S(1)} all-to-all(f32[64,256,8]{1,0,2:T(8,128)S(1)} %copy.27), channel_id=1, replica_groups=mesh['row'=4,'col'=8] {'col'}, dimensions={2} | all-to-all | bytes 1048576 | tf_op jit(solution)/shard_map/all_to_all | solution.py:20
  191.8 9.3 %reduce.5 = f32[2048,64]{1,0:T(8,128)S(1)} reduce(f32[2048,1,64]{2,1,0:T(1,128)S(1)} %bitcast.76, f32[]{:T(128)} %broadcast.24), dimensions={1}, to_apply=%bitcast.66.reduce_sub_computation | reduce | bytes 1048580
  201.1 0.7 reshape.50
  201.8 16.6 %all_to_all.111 = f32[4,1,32768]{2,1,0:T(1,128)S(1)} all-to-all(f32[4,1,32768]{2,1,0:T(1,128)S(1)} %reshape.50), channel_id=1, replica_groups=mesh['row'=4,'col'=8] {'row'}, dimensions={0} | all-to-all | bytes 1048576 | tf_op jit(solution)/shard_map/all_to_all | solution.py:21
  218.4 2.1 reduce.6
  220.5 1.3 reshape.51
  222.2 1.0 copy.31
  223.4 34.3 %all-gather.7.cloned.1.call-done = f32[256,512,8]{1,0,2:T(8,128)} async-done(((f32[256,512,1]{1,0,2:T(8,128)}), f32[256,512,8]{1,0,2:T(8,128)}) %all-gather.7.cloned.1.call-update) | async-done | bytes 4194320 | tf_op jit(solution)/shard_map/all_gather | solution.py:22
  257.7 5.5 copy.32
  263.2 33.8 %fusion.5 = f32[256,2048]{1,0:T(8,128)} fusion(f32[4096,2048]{1,0:T(8,128)} %param.4, f32[256,512,8]{0,2,1:T(8,128)} %copy.32), kind=kOutput, calls=%fused_computation.6 | convolution fusion | flops 25769803776 | bytes 39845888 | tf_op jit(solution)/shard_map/dot_general | solution.py:33
  297.2 0.5 all-gather.11.cloned.1.call-update
  297.8 43.2 %reduce-scatter.6.cloned.1.call-done = f32[64,2048]{1,0:T(8,128)} async-done(((f32[256,2048]{1,0:T(8,128)}), f32[64,2048]{1,0:T(8,128)}) %reduce-scatter.6.cloned.1.call-update) | async-done | bytes 524304 | tf_op jit(solution)/shard_map/reduce_scatter | solution.py:36
  340.9 2.0 broadcast_multiply_fusion
  343.3 0.4 copy.34
  343.7 13.5 %all_to_all.112 = f32[64,256,8]{1,0,2:T(8,128)} all-to-all(f32[64,256,8]{1,0,2:T(8,128)S(1)} %copy.34), channel_id=1, replica_groups=mesh['row'=4,'col'=8] {'col'}, dimensions={2} | all-to-all | bytes 1048576 | tf_op jit(solution)/shard_map/all_to_all | solution.py:20
  357.2 1.4 copy.47
  358.5 10.3 %reduce.7 = f32[2048,64]{1,0:T(8,128)} reduce(f32[2048,1,64]{2,1,0:T(1,128)S(1)} %bitcast.77, f32[]{:T(128)} %broadcast.24), dimensions={1}, to_apply=%bitcast.68.reduce_sub_computation | reduce | bytes 1048580
  368.9 1.9 reshape.52
  370.7 32.0 %all_to_all.113 = f32[4,1,32768]{2,1,0:T(1,128)S(1)} all-to-all(f32[4,1,32768]{2,1,0:T(1,128)S(1)} %reshape.52), channel_id=1, replica_groups=mesh['row'=4,'col'=8] {'row'}, dimensions={0} | all-to-all | bytes 1048576 | tf_op jit(solution)/shard_map/all_to_all | solution.py:21
  402.7 2.1 reduce.8
  404.8 1.3 reshape.53
  406.5 1.0 copy.38
  407.8 2.6 reduce_sum.29
  410.7 57.2 %all-gather.11.cloned.1.call-done = f32[3,256,2048]{2,1,0:T(8,128)} async-done(((f32[3,64,2048]{2,1,0:T(8,128)}), f32[3,256,2048]{2,1,0:T(8,128)}) %all-gather.11.cloned.1.call-update) | async-done | bytes 6291472 | tf_op jit(solution)/shard_map/all_gather | solution.py:13
  468.0 32.4 %fusion.7 = f32[4096,2048]{1,0:T(8,128)} fusion(f32[256,512,8]{0,2,1:T(8,128)} %copy.25, f32[3,256,2048]{2,1,0:T(8,128)} %all-gather.11.cloned.1.call-done), kind=kOutput, calls=%fused_computation.8 | convolution fusion | flops 25769803776 | bytes 39845888 | tf_op jit(solution)/shard_map/dot_general | solution.py:26
  500.4 2.7 reduce_sum.28
  503.4 32.7 %fusion.3 = f32[4096,2048]{1,0:T(8,128)} fusion(f32[256,512,8]{0,2,1:T(8,128)} %copy.32, f32[3,256,2048]{2,1,0:T(8,128)} %all-gather.11.cloned.1.call-done), kind=kOutput, calls=%fused_computation.4 | convolution fusion | flops 25769803776 | bytes 39845888 | tf_op jit(solution)/shard_map/dot_general | solution.py:26
  536.0 2.6 reduce_sum.27
  539.0 5.5 copy.39
  544.4 33.9 %fusion.1 = f32[256,2048]{1,0:T(8,128)} fusion(f32[4096,2048]{1,0:T(8,128)} %param.4, f32[256,512,8]{0,2,1:T(8,128)} %copy.39), kind=kOutput, calls=%fused_computation.2 | convolution fusion | flops 25769803776 | bytes 39845888 | tf_op jit(solution)/shard_map/dot_general | solution.py:33
  578.4 0.7 pad_maximum_fusion
  579.1 46.4 %add_add_fusion = f32[4096,2048]{1,0:T(8,128)} fusion(f32[4096,2048]{1,0:T(8,128)} %fusion.7, f32[4096,2048]{1,0:T(8,128)} %fusion.3, f32[256,512,8]{0,2,1:T(8,128)} %copy.39, f32[3,256,2048]{2,1,0:T(8,128)} %all-gather.11.cloned.1.call-done), kind=kOutput, calls=%fused_computation | convolution fusion | flops 25786580992 | bytes 106954752 | tf_op jit(solution)/shard_map/dot_general | solution.py:26
  625.4 1.9 fusion.11
  (41 shorter events, 5.1 us)
Async XLA Ops:
  7.2 85.4 %all-gather.5.cloned.1.call-start = ((), (), s32[]{:S(2)}) async-start(), calls=%async_computation.9 | async-start | bytes 4718592 | tf_op jit(solution)/shard_map/all_gather | solution.py:22
  58.0 117.7 %reduce-scatter.4.cloned.1.call-start = ((), (), s32[]{:S(2)}) async-start(), calls=%async_computation.10 | async-start | bytes 2621440 | tf_op jit(solution)/shard_map/reduce_scatter | solution.py:36
  98.0 33.9 %copy-start.4 = (f32[2048]{0:T(1024)S(1)}, f32[2048]{0:T(1024)}, u32[]{:S(2)}) copy-start(f32[2048]{0:T(1024)} %param.5) | copy-start | bytes 24580
  98.0 77.7 %copy-start.1 = (f32[64,2048]{1,0:T(8,128)S(1)}, f32[64,2048]{1,0:T(8,128)}, u32[]{:S(2)}) copy-start(f32[64,2048]{1,0:T(8,128)} %param.7) | copy-start | bytes 1572868
  131.9 125.9 %all-gather.7.cloned.1.call-start = ((), (), s32[]{:S(2)}) async-start(), calls=%async_computation.11 | async-start | bytes 4718592 | tf_op jit(solution)/shard_map/all_gather | solution.py:22
  223.2 117.7 %reduce-scatter.6.cloned.1.call-start = ((), (), s32[]{:S(2)}) async-start(), calls=%async_computation.12 | async-start | bytes 2621440 | tf_op jit(solution)/shard_map/reduce_scatter | solution.py:36
  263.2 77.7 %copy-start.3 = (f32[64,2048]{1,0:T(8,128)S(1)}, f32[64,2048]{1,0:T(8,128)}, u32[]{:S(2)}) copy-start(f32[64,2048]{1,0:T(8,128)} %reduce-scatter.4.cloned.1.call-done) | copy-start | bytes 1572868
  297.1 43.8 %copy-start = (f32[3,64,2048]{2,1,0:T(8,128)S(1)}, f32[3,64,2048]{2,1,0:T(8,128)}, u32[]{:S(2)}) copy-start(f32[3,64,2048]{2,1,0:T(8,128)} %param.6) | copy-start | bytes 4718596
  297.1 170.9 %all-gather.11.cloned.1.call-start = ((), (), s32[]{:S(2)}) async-start(), calls=%async_computation.15 | async-start | bytes 7864320 | tf_op jit(solution)/shard_map/all_gather | solution.py:13
  297.7 238.3 %all-gather.9.cloned.1.call-start = ((), (), s32[]{:S(2)}) async-start(), calls=%async_computation.13 | async-start | bytes 4718592 | tf_op jit(solution)/shard_map/all_gather | solution.py:22
  407.5 217.9 %reduce-scatter.8.cloned.1.call-start = ((), (), s32[]{:S(2)}) async-start(), calls=%async_computation.14 | async-start | bytes 2621440 | tf_op jit(solution)/shard_map/reduce_scatter | solution.py:36
  579.1 46.4 %copy-start.2 = (f32[64,2048]{1,0:T(8,128)S(1)}, f32[64,2048]{1,0:T(8,128)}, u32[]{:S(2)}) copy-start(f32[64,2048]{1,0:T(8,128)} %get-tuple-element.4) | copy-start | bytes 1572868
Sparse Core Ops, SparseCore 0:
  58.1 34.4 all-gather.4
  132.0 43.6 reduce-scatter.3
  223.3 34.4 all-gather.6
  297.2 43.6 reduce-scatter.5
  342.3 125.6 all-gather.10
  469.7 34.7 all-gather.8
  578.5 41.7 reduce-scatter.7
where the time goes:
time: 642 us; the launch traced here: 634 us
  waiting for transfers between devices  213 us (33%)
  matrix products  213 us (33%)
  blocking collectives  109 us (17%)
  other arithmetic  50.4 us (8%)
  local copies, waits for them, and re-layouts  33 us (5%)
  between operations  14.6 us (2%)
    dot_general x3, matrix products, shards(): lax.dot_general(unit_block, rates_now, (((0,), (0,)), ((), ())), precisio...  111 us
    dot_general x3, matrix products, shards(): jnp.dot(unit_block, weight, precision=lax.Precision.HIGHEST, preferred_el...  102 us
    reduce_scatter x3, waiting for transfers between devices, shards(): lax.psum_scatter(partial_sum, 'row', scatter_dimension=0, tiled=True)  86.9 us
    all_gather x3, waiting for transfers between devices, shards(): gathered = lax.all_gather(by_row, 'col', axis=2, tiled=True)  68.6 us
    all_to_all x3, blocking collectives, shards(): lax.all_to_all(by_col, 'row', split_axis=1, concat_axis=0, tiled=True)  67.2 us
    all_gather x1, waiting for transfers between devices, shards(): full_rates = lax.all_gather(rates, 'row', axis=1, tiled=True)  57.2 us
    all_to_all x3, blocking collectives, shards(): lax.all_to_all(spread, 'col', split_axis=2, concat_axis=1, tiled=True)  41.9 us
    unnamed x3, other arithmetic  29 us
  transfers between devices with their start and end apart: 7, of which 5 were waited for; matrix products, arithmetic and copies ran while one was open for 22% of the time, Pallas kernels for 0%

commit v1 on v0

--- a/solution.py
+++ b/solution.py
@@ -19,7 +19,8 @@
         spread = scaled.reshape(own_rows, local_units // n_col, n_col)
         by_col = lax.all_to_all(spread, "col", split_axis=2, concat_axis=1, tiled=True)
         by_row = lax.all_to_all(by_col, "row", split_axis=1, concat_axis=0, tiled=True)
-        gathered = lax.all_gather(by_row, "col", axis=2, tiled=True)
+        val = lax.all_gather(by_row, "col")
+        gathered = jnp.concatenate(val, axis=2)
         unit_block = gathered.reshape(gathered.shape[0], gathered.shape[1] * gathered.shape[2])
         rates_now = full_rates[step_back]
         noise_list.insert(0, jnp.sum(unit_block, axis=0))

time: 642 us -> 640 us (level)
  no operation moved by 1% of the time
where the time goes in v1:
time: 640 us; the launch traced here: 632 us
  waiting for transfers between devices  213 us (33%)
  matrix products  212 us (33%)
  blocking collectives  109 us (17%)
  other arithmetic  48.9 us (8%)
  local copies, waits for them, and re-layouts  33.1 us (5%)
  between operations  14.6 us (2%)
    dot_general x3, matrix products, shards(): lax.dot_general(unit_block, rates_now, (((0,), (0,)), ((), ())), precisio...  112 us
    dot_general x3, matrix products, shards(): jnp.dot(unit_block, weight, precision=lax.Precision.HIGHEST, preferred_el...  101 us
    reduce_scatter x3, waiting for transfers between devices, shards(): lax.psum_scatter(partial_sum, 'row', scatter_dimension=0, tiled=True)  86.8 us
    all_gather x3, waiting for transfers between devices, shards(): val = lax.all_gather(by_row, 'col')  68.6 us
    all_to_all x3, blocking collectives, shards(): lax.all_to_all(by_col, 'row', split_axis=1, concat_axis=0, tiled=True)  67.2 us
    all_gather x1, waiting for transfers between devices, shards(): full_rates = lax.all_gather(rates, 'row', axis=1, tiled=True)  57.2 us
    all_to_all x3, blocking collectives, shards(): lax.all_to_all(spread, 'col', split_axis=2, concat_axis=1, tiled=True)  41.9 us
    unnamed x3, other arithmetic  29 us
  transfers between devices with their start and end apart: 7, of which 5 were waited for; matrix products, arithmetic and copies ran while one was open for 22% of the time, Pallas kernels for 0%

profile of v1, /device:TPU:0, one launch (start us, length us, event | category | flops | bytes accessed | tf_op | source)
XLA Modules:
  0.0 632.0 jit_solution(6161665524848957625)
XLA Ops:
  7.2 1.1 broadcast_multiply_fusion.2
  8.6 0.4 copy.20
  9.0 14.7 %all_to_all.99 = f32[64,256,8]{1,0,2:T(8,128)S(1)} all-to-all(f32[64,256,8]{1,0,2:T(8,128)S(1)} %copy.20), channel_id=1, replica_groups=mesh['row'=4,'col'=8] {'col'}, dimensions={2} | all-to-all | bytes 1048576 | tf_op jit(solution)/shard_map/all_to_all | solution.py:20
  24.1 0.5 broadcast.24
  24.6 9.3 %reduce.3 = f32[2048,64]{1,0:T(8,128)S(1)} reduce(f32[2048,1,64]{2,1,0:T(1,128)S(1)} %bitcast.84, f32[]{:T(128)} %broadcast.24), dimensions={1}, to_apply=%bitcast.73.reduce_sub_computation | reduce | bytes 1048580
  33.9 0.7 reshape.51
  34.6 18.6 %all_to_all.100 = f32[4,1,32768]{2,1,0:T(1,128)S(1)} all-to-all(f32[4,1,32768]{2,1,0:T(1,128)S(1)} %reshape.51), channel_id=1, replica_groups=mesh['row'=4,'col'=8] {'row'}, dimensions={0} | all-to-all | bytes 1048576 | tf_op jit(solution)/shard_map/all_to_all | solution.py:21
  53.2 2.1 reduce.4
  55.3 1.3 reshape.52
  57.0 1.0 copy.24
  58.3 34.2 %all-gather.5.cloned.1.call-done = f32[8,256,512,1]{2,1,3,0:T(8,128)} async-done(((f32[1,256,512,1]{2,1,3,0:T(8,128)}), f32[8,256,512,1]{2,1,3,0:T(8,128)}) %all-gather.5.cloned.1.call-update) | async-done | bytes 4194320 | tf_op jit(solution)/shard_map/all_gather | solution.py:22
  92.6 5.4 copy.25
  98.0 33.8 %fusion.9 = f32[256,2048]{1,0:T(8,128)} fusion(f32[4096,2048]{1,0:T(8,128)} %param.4, f32[8,256,512,1]{1,0,2,3:T(8,128)} %copy.25), kind=kOutput, calls=%fused_computation.10 | convolution fusion | flops 25769803776 | bytes 39845888 | tf_op jit(solution)/shard_map/dot_general | solution.py:34
  132.0 43.7 %reduce-scatter.4.cloned.1.call-done = f32[64,2048]{1,0:T(8,128)} async-done(((f32[256,2048]{1,0:T(8,128)}), f32[64,2048]{1,0:T(8,128)}) %reduce-scatter.4.cloned.1.call-update) | async-done | bytes 524304 | tf_op jit(solution)/shard_map/reduce_scatter | solution.py:37
  175.7 1.3 broadcast_multiply_fusion.1
  177.7 13.7 %all_to_all.101 = f32[64,256,8]{1,0,2:T(8,128)S(1)} all-to-all(f32[64,256,8]{1,0,2:T(8,128)S(1)} %copy.27), channel_id=1, replica_groups=mesh['row'=4,'col'=8] {'col'}, dimensions={2} | all-to-all | bytes 1048576 | tf_op jit(solution)/shard_map/all_to_all | solution.py:20
  191.7 9.3 %reduce.5 = f32[2048,64]{1,0:T(8,128)S(1)} reduce(f32[2048,1,64]{2,1,0:T(1,128)S(1)} %bitcast.85, f32[]{:T(128)} %broadcast.24), dimensions={1}, to_apply=%bitcast.75.reduce_sub_computation | reduce | bytes 1048580
  201.1 0.7 reshape.53
  201.8 16.6 %all_to_all.102 = f32[4,1,32768]{2,1,0:T(1,128)S(1)} all-to-all(f32[4,1,32768]{2,1,0:T(1,128)S(1)} %reshape.53), channel_id=1, replica_groups=mesh['row'=4,'col'=8] {'row'}, dimensions={0} | all-to-all | bytes 1048576 | tf_op jit(solution)/shard_map/all_to_all | solution.py:21
  218.4 2.1 reduce.6
  220.5 1.3 reshape.54
  222.2 1.0 copy.31
  223.4 34.3 %all-gather.7.cloned.1.call-done = f32[8,256,512,1]{2,1,3,0:T(8,128)} async-done(((f32[1,256,512,1]{2,1,3,0:T(8,128)}), f32[8,256,512,1]{2,1,3,0:T(8,128)}) %all-gather.7.cloned.1.call-update) | async-done | bytes 4194320 | tf_op jit(solution)/shard_map/all_gather | solution.py:22
  257.8 5.5 copy.32
  263.2 33.9 %fusion.5 = f32[256,2048]{1,0:T(8,128)} fusion(f32[4096,2048]{1,0:T(8,128)} %param.4, f32[8,256,512,1]{1,0,2,3:T(8,128)} %copy.32), kind=kOutput, calls=%fused_computation.6 | convolution fusion | flops 25769803776 | bytes 39845888 | tf_op jit(solution)/shard_map/dot_general | solution.py:34
  297.2 0.5 all-gather.11.cloned.1.call-update
  297.8 43.1 %reduce-scatter.6.cloned.1.call-done = f32[64,2048]{1,0:T(8,128)} async-done(((f32[256,2048]{1,0:T(8,128)}), f32[64,2048]{1,0:T(8,128)}) %reduce-scatter.6.cloned.1.call-update) | async-done | bytes 524304 | tf_op jit(solution)/shard_map/reduce_scatter | solution.py:37
  340.9 2.0 broadcast_multiply_fusion
  343.7 13.5 %all_to_all.103 = f32[64,256,8]{1,0,2:T(8,128)} all-to-all(f32[64,256,8]{1,0,2:T(8,128)S(1)} %copy.34), channel_id=1, replica_groups=mesh['row'=4,'col'=8] {'col'}, dimensions={2} | all-to-all | bytes 1048576 | tf_op jit(solution)/shard_map/all_to_all | solution.py:20
  357.1 1.4 copy.50
  358.5 10.3 %reduce.7 = f32[2048,64]{1,0:T(8,128)} reduce(f32[2048,1,64]{2,1,0:T(1,128)S(1)} %bitcast.86, f32[]{:T(128)} %broadcast.24), dimensions={1}, to_apply=%bitcast.77.reduce_sub_computation | reduce | bytes 1048580
  368.8 1.9 reshape.55
  370.7 32.0 %all_to_all.104 = f32[4,1,32768]{2,1,0:T(1,128)S(1)} all-to-all(f32[4,1,32768]{2,1,0:T(1,128)S(1)} %reshape.55), channel_id=1, replica_groups=mesh['row'=4,'col'=8] {'row'}, dimensions={0} | all-to-all | bytes 1048576 | tf_op jit(solution)/shard_map/all_to_all | solution.py:21
  402.7 2.1 reduce.8
  404.8 1.3 reshape.56
  406.5 1.0 copy.38
  407.8 2.8 bitcast_reduce_fusion.2
  410.8 57.2 %all-gather.11.cloned.1.call-done = f32[3,256,2048]{2,1,0:T(8,128)} async-done(((f32[3,64,2048]{2,1,0:T(8,128)}), f32[3,256,2048]{2,1,0:T(8,128)}) %all-gather.11.cloned.1.call-update) | async-done | bytes 6291472 | tf_op jit(solution)/shard_map/all_gather | solution.py:13
  468.0 32.5 %fusion.7 = f32[4096,2048]{1,0:T(8,128)} fusion(f32[8,256,512,1]{1,0,2,3:T(8,128)} %copy.25, f32[3,256,2048]{2,1,0:T(8,128)} %all-gather.11.cloned.1.call-done), kind=kOutput, calls=%fused_computation.8 | convolution fusion | flops 25769803776 | bytes 39845888 | tf_op jit(solution)/shard_map/dot_general | solution.py:27
  500.5 0.6 bitcast_reduce_fusion.1
  501.3 32.7 %fusion.3 = f32[4096,2048]{1,0:T(8,128)} fusion(f32[8,256,512,1]{1,0,2,3:T(8,128)} %copy.32, f32[3,256,2048]{2,1,0:T(8,128)} %all-gather.11.cloned.1.call-done), kind=kOutput, calls=%fused_computation.4 | convolution fusion | flops 25769803776 | bytes 39845888 | tf_op jit(solution)/shard_map/dot_general | solution.py:27
  534.0 5.5 copy.39
  539.5 3.0 bitcast_reduce_fusion
  542.5 0.5 copy-done
  543.0 32.8 %fusion.1 = f32[256,2048]{1,0:T(8,128)} fusion(f32[4096,2048]{1,0:T(8,128)} %param.4, f32[8,256,512,1]{1,0,2,3:T(8,128)S(1)} %copy-done), kind=kOutput, calls=%fused_computation.2 | convolution fusion | flops 25769803776 | bytes 39845888 | tf_op jit(solution)/shard_map/dot_general | solution.py:34
  576.0 0.7 pad_maximum_fusion
  576.7 46.3 %add_add_fusion = f32[4096,2048]{1,0:T(8,128)} fusion(f32[4096,2048]{1,0:T(8,128)} %fusion.7, f32[4096,2048]{1,0:T(8,128)} %fusion.3, f32[8,256,512,1]{1,0,2,3:T(8,128)} %copy.39, f32[3,256,2048]{2,1,0:T(8,128)} %all-gather.11.cloned.1.call-done), kind=kOutput, calls=%fused_computation | convolution fusion | flops 25786580992 | bytes 106954752 | tf_op jit(solution)/shard_map/dot_general | solution.py:27
  623.0 1.9 fusion.11
  (42 shorter events, 5.1 us)
Async XLA Ops:
  7.2 85.4 %all-gather.5.cloned.1.call-start = ((), (), s32[]{:S(2)}) async-start(), calls=%async_computation.9 | async-start | bytes 4718592 | tf_op jit(solution)/shard_map/all_gather | solution.py:22
  58.0 117.7 %reduce-scatter.4.cloned.1.call-start = ((), (), s32[]{:S(2)}) async-start(), calls=%async_computation.10 | async-start | bytes 2621440 | tf_op jit(solution)/shard_map/reduce_scatter | solution.py:37
  98.0 33.9 %copy-start.6 = (f32[2048]{0:T(1024)S(1)}, f32[2048]{0:T(1024)}, u32[]{:S(2)}) copy-start(f32[2048]{0:T(1024)} %param.5) | copy-start | bytes 24580
  98.0 77.7 %copy-start.3 = (f32[64,2048]{1,0:T(8,128)S(1)}, f32[64,2048]{1,0:T(8,128)}, u32[]{:S(2)}) copy-start(f32[64,2048]{1,0:T(8,128)} %param.7) | copy-start | bytes 1572868
  131.9 125.9 %all-gather.7.cloned.1.call-start = ((), (), s32[]{:S(2)}) async-start(), calls=%async_computation.11 | async-start | bytes 4718592 | tf_op jit(solution)/shard_map/all_gather | solution.py:22
  223.2 117.7 %reduce-scatter.6.cloned.1.call-start = ((), (), s32[]{:S(2)}) async-start(), calls=%async_computation.12 | async-start | bytes 2621440 | tf_op jit(solution)/shard_map/reduce_scatter | solution.py:37
  263.2 77.6 %copy-start.5 = (f32[64,2048]{1,0:T(8,128)S(1)}, f32[64,2048]{1,0:T(8,128)}, u32[]{:S(2)}) copy-start(f32[64,2048]{1,0:T(8,128)} %reduce-scatter.4.cloned.1.call-done) | copy-start | bytes 1572868
  297.1 43.8 %copy-start.2 = (f32[3,64,2048]{2,1,0:T(8,128)S(1)}, f32[3,64,2048]{2,1,0:T(8,128)}, u32[]{:S(2)}) copy-start(f32[3,64,2048]{2,1,0:T(8,128)} %param.6) | copy-start | bytes 4718596
  297.1 170.9 %all-gather.11.cloned.1.call-start = ((), (), s32[]{:S(2)}) async-start(), calls=%async_computation.15 | async-start | bytes 7864320 | tf_op jit(solution)/shard_map/all_gather | solution.py:13
  297.7 236.3 %all-gather.9.cloned.1.call-start = ((), (), s32[]{:S(2)}) async-start(), calls=%async_computation.13 | async-start | bytes 4718592 | tf_op jit(solution)/shard_map/all_gather | solution.py:22
  407.5 215.5 %reduce-scatter.8.cloned.1.call-start = ((), (), s32[]{:S(2)}) async-start(), calls=%async_computation.14 | async-start | bytes 2621440 | tf_op jit(solution)/shard_map/reduce_scatter | solution.py:37
  468.0 32.5 %copy-start.1 = (f32[8,256,512,1]{1,0,2,3:T(8,128)S(1)}, f32[8,256,512,1]{1,0,2,3:T(8,128)}, u32[]{:S(2)}) copy-start(f32[8,256,512,1]{1,0,2,3:T(8,128)} %copy.32) | copy-start | bytes 12582916
  539.5 3.4 copy-start
  576.7 46.3 %copy-start.4 = (f32[64,2048]{1,0:T(8,128)S(1)}, f32[64,2048]{1,0:T(8,128)}, u32[]{:S(2)}) copy-start(f32[64,2048]{1,0:T(8,128)} %get-tuple-element.4) | copy-start | bytes 1572868
Sparse Core Ops, SparseCore 0:
  58.1 34.4 all-gather.4
  132.0 43.6 reduce-scatter.3
  223.3 34.4 all-gather.6
  297.2 43.5 reduce-scatter.5
  342.3 125.6 all-gather.10
  469.7 34.7 all-gather.8
  576.1 41.8 reduce-scatter.7
